TPU v7x, 128 devices: a whole 4x4x4 slice. The times are simulated.
128 devices in a mesh: row: 8 (over z, core), col: 16 (over x, y).
Axes of the slice: x: 4, y: 4, z: 4, core: 2. Of those that a mesh axis runs over, the one named last changes fastest.
Arguments:
- tile_values: float32 [2048, 512, 512], P(('row', 'col')), may hold values from -6 to 6
- tile_coords: int32 [2048, 2], P(('row', 'col')), may hold values from 0 to 3, as said below
- tile_counts: int32 [128], P(('row', 'col')), may hold values from 4 to 16, as said below
- restrict_basis: float32 [16384, 256], P(('row', 'col')), may hold values from -0.25 to 0.25
- prolong_basis: float32 [32768, 256], P(('col', 'row')), may hold values from -0.25 to 0.25
- row_partner: int32 [16, 8], replicated, may hold values from 0 to 7, as said below
- col_partner: int32 [8, 16], replicated, may hold values from 0 to 15, as said below
Outputs:
- coarse: float32 [4096, 8192], P('row', 'col')
Inputs may be any that keep to these rules, and one draw needn't show every extreme that they name: `tile_coords`: within one device's 16 slots no two name the same (block row, block column); first entry below 4, second below 4; dead slots also hold such positions. `tile_counts`: number of leading slots of each device that are live; some device has all 16 live. `row_partner`: each row is a pairing: the partner of a part's partner is the part itself, never the part. `col_partner`: each row is a pairing: the partner of a part's partner is the part itself, never the part.
All inputs are finite; a program needn't handle non-finite values.
Results may differ from a plain program's by a relative error of at most 0.0003.
Values sent between devices are 32-bit elements; how exact they have to be, the bound alone decides.
A program may use at most 128 MiB of HBM per device.

v0:
```python
import jax
import jax.numpy as jnp
from jax import lax
from jax.sharding import PartitionSpec as P


def pick_half(block, keep_flag, axis_dim):
    half_size = block.shape[axis_dim] // 2
    first = lax.slice_in_dim(block, 0, half_size, 1, axis_dim)
    second = lax.slice_in_dim(block, half_size, 2 * half_size, 1, axis_dim)
    kept = jnp.where(keep_flag, second, first)
    given = jnp.where(keep_flag, first, second)
    return (kept, given)


def body(
    tile_values, tile_coords, tile_counts, restrict_basis, prolong_basis, row_partner, col_partner
):
    restrict_part = lax.all_gather(restrict_basis, "col", axis=0, tiled=True)
    prolong_part = lax.all_gather(prolong_basis, "row", axis=0, tiled=True)
    tile_order = tile_values.shape[1]
    basis_width = restrict_basis.shape[1]
    block_rows = restrict_part.shape[0] // tile_order
    block_cols = prolong_part.shape[0] // tile_order
    live_count = tile_counts[0]

    def add_slot(slot_index, grid_now):
        block_row = tile_coords[slot_index, 0]
        block_col = tile_coords[slot_index, 1]
        left = lax.dynamic_slice_in_dim(restrict_part, block_row * tile_order, tile_order, 0)
        right = lax.dynamic_slice_in_dim(prolong_part, block_col * tile_order, tile_order, 0)
        applied = jnp.dot(tile_values[slot_index], right, precision=lax.Precision.HIGHEST)
        product = jnp.dot(left.T, applied, precision=lax.Precision.HIGHEST)
        product = jnp.where(slot_index < live_count, product, jnp.zeros_like(product))
        place = (block_row * basis_width, block_col * basis_width)
        current = lax.dynamic_slice(grid_now, place, (basis_width, basis_width))
        return lax.dynamic_update_slice(grid_now, current + product, place)

    start_grid = jnp.zeros((block_rows * basis_width, block_cols * basis_width), jnp.float32)
    local_grid = lax.fori_loop(0, tile_values.shape[0], add_slot, start_grid)
    my_row = lax.axis_index("row")
    my_col = lax.axis_index("col")
    row_table = row_partner[my_col]
    col_table = col_partner[my_row]
    partner_row = row_table[my_row]
    partner_col = col_table[my_col]
    keep_row = my_row > partner_row
    keep_col = my_col > partner_col
    kept, given = pick_half(local_grid, keep_row, 0)
    height = kept.shape[0]
    gathered = lax.all_gather(given, "row", axis=0, tiled=True)
    incoming = lax.dynamic_slice_in_dim(gathered, partner_row * height, height, 0)
    row_section = kept + incoming
    kept, given = pick_half(row_section, keep_col, 1)
    breadth = kept.shape[1]
    gathered = lax.all_gather(given, "col", axis=1, tiled=True)
    incoming = lax.dynamic_slice_in_dim(gathered, partner_col * breadth, breadth, 1)
    return kept + incoming


def solution(mesh):
    in_specs = (
        P(("row", "col"), None, None),
        P(("row", "col"), None),
        P(("row", "col")),
        P(("row", "col"), None),
        P(("col", "row"), None),
        P(),
        P(),
    )
    out_specs = P("row", "col")
    return jax.shard_map(body, mesh=mesh, in_specs=in_specs, out_specs=out_specs, check_vma=False)
```

profile of v0, /device:TPU:1, one launch (start us, length us, event | category | flops | bytes accessed | tf_op | source)
XLA Modules:
  0.0 450.1 jit_solution(11749270185741397715)
XLA Ops:
  10.1 28.1 %all-gather.7.cloned.1.call-done = f32[2048,256]{1,0:T(8,128)} async-done(((f32[256,256]{1,0:T(8,128)}), f32[2048,256]{1,0:T(8,128)}) %all-gather.7.cloned.1.call-update) | async-done | bytes 2097168 | tf_op jit(solution)/shard_map/all_gather | solution.py:20
  38.2 45.2 %all-gather.5.cloned.1.call-done = f32[2048,256]{1,0:T(8,128)} async-done(((f32[128,256]{1,0:T(8,128)}), f32[2048,256]{1,0:T(8,128)}) %all-gather.5.cloned.1.call-update) | async-done | bytes 2097168 | tf_op jit(solution)/shard_map/all_gather | solution.py:19
  85.9 148.6 %while.13 = (s32[]{:T(128)}, f32[1024,1024]{1,0:T(8,128)}, s32[16,2]{0,1:T(2,128)S(1)}, s32[]{:T(128)}, f32[2048,256]{1,0:T(8,128)}, /*index=5*/f32[16,512,512]{...) while((s32[]{:T(128)}, f32[1024,1024]{1,0:T(8,128)}, ...), condition=%wide.region_1.2_spmd, body=%wide.region_0.1_spmd.sunk | while | flops 1208090624 | bytes 3670383 | solution.py:40
  92.3 2.9 fusion.21
  101.6 2.9 fusion.21
  110.9 2.9 fusion.21
  120.2 2.9 fusion.21
  129.4 2.9 fusion.21
  138.7 2.8 fusion.21
  148.0 2.9 fusion.21
  157.3 2.9 fusion.21
  166.6 2.9 fusion.21
  175.9 2.9 fusion.21
  185.2 2.9 fusion.21
  194.5 2.9 fusion.21
  203.7 2.8 fusion.21
  213.0 2.9 fusion.21
  222.3 2.9 fusion.21
  231.6 2.8 fusion.21
  234.4 4.1 slice_select_fusion
  241.3 83.9 %all-gather.9.cloned.1.call-done = f32[4096,1024]{1,0:T(8,128)} async-done(((f32[512,1024]{1,0:T(8,128)}), f32[4096,1024]{1,0:T(8,128)}) %all-gather.9.cloned.1.call-update) | async-done | bytes 16777232 | tf_op jit(solution)/shard_map/all_gather | solution.py:51
  325.2 3.5 dynamic-slice_add_fusion
  330.6 110.5 %all-gather.11.cloned.1.call-done = f32[512,8192]{1,0:T(8,128)} async-done(((f32[512,512]{1,0:T(8,128)}), f32[512,8192]{1,0:T(8,128)}) %all-gather.11.cloned.1.call-update) | async-done | bytes 16777232 | tf_op jit(solution)/shard_map/all_gather | solution.py:56
  441.0 2.5 dynamic-slice_add_fusion.1
  (46 shorter events, 56.2 us)
Async XLA Ops:
  6.5 31.7 %all-gather.7.cloned.1.call-start = ((), (), s32[]{:S(2)}) async-start(), calls=%async_computation.1 | async-start | bytes 2359296 | tf_op jit(solution)/shard_map/all_gather | solution.py:20
  7.3 76.1 %all-gather.5.cloned.1.call-start = ((), (), s32[]{:S(2)}) async-start(), calls=%async_computation | async-start | bytes 2228224 | tf_op jit(solution)/shard_map/all_gather | solution.py:19
  8.0 317.2 %all-gather.9.cloned.1.call-start = ((), (), s32[]{:S(2)}) async-start(), calls=%async_computation.2 | async-start | bytes 18874368 | tf_op jit(solution)/shard_map/all_gather | solution.py:51
  83.4 2.5 copy-start
  238.6 202.4 %all-gather.11.cloned.1.call-start = ((), (), s32[]{:S(2)}) async-start(), calls=%async_computation.3 | async-start | bytes 17825792 | tf_op jit(solution)/shard_map/all_gather | solution.py:56
Sparse Core Ops, SparseCore 0:
  9.0 29.1 all-gather.6
  40.3 43.0 all-gather.4
  238.7 86.4 all-gather.8
  330.1 110.9 all-gather.10
where the time goes:
time: 452 us; the launch traced here: 450 us
  waiting for transfers between devices  269 us (60%)
  matrix products  83.4 us (18%)
  loops' own time  54.4 us (12%)
  local copies, waits for them, and re-layouts  15.9 us (4%)
  between operations  15.8 us (3%)
  other arithmetic  11.4 us (3%)
    all_gather x1, waiting for transfers between devices, body(): gathered = lax.all_gather(given, 'col', axis=1, tiled=True)  110 us
    all_gather x1, waiting for transfers between devices, body(): gathered = lax.all_gather(given, 'row', axis=0, tiled=True)  83.9 us
    another operation x1, loops' own time, body(): local_grid = lax.fori_loop(0, tile_values.shape[0], add_slot, start_grid)  54.4 us
    dot_general x16, matrix products, add_slot(): product = jnp.dot(left.T, applied, precision=lax.Precision.HIGHEST)  45.9 us
    all_gather x1, waiting for transfers between devices, body(): restrict_part = lax.all_gather(restrict_basis, 'col', axis=0, tiled=True)  45.2 us
    dot_general x16, matrix products, add_slot(): jnp.dot(tile_values[slot_index], right, precision=lax.Precision.HIGHEST)  37.6 us
    all_gather x1, waiting for transfers between devices, body(): prolong_part = lax.all_gather(prolong_basis, 'row', axis=0, tiled=True)  28.1 us
    dynamic_slice x16, local copies, waits for them, and re-layouts, add_slot(): block_col = tile_coords[slot_index, 1]  10.7 us
  transfers between devices with their start and end apart: 4, of which 4 were waited for; matrix products, arithmetic and copies ran while one was open for 1% of the time, Pallas kernels for 0%

commit v1 on v0

--- a/solution.py
+++ b/solution.py
@@ -53,7 +53,9 @@
     row_section = kept + incoming
     kept, given = pick_half(row_section, keep_col, 1)
     breadth = kept.shape[1]
-    gathered = lax.all_gather(given, "col", axis=1, tiled=True)
+    gathered = jnp.concatenate(
+        lax.all_to_all(jnp.stack([given] * lax.axis_size("col")), "col", 0, 0), axis=1
+    )
     incoming = lax.dynamic_slice_in_dim(gathered, partner_col * breadth, breadth, 1)
     return kept + incoming
 

time: 452 us -> 729 us (1.61)
  waiting for transfers between devices: 269 us -> 456 us
  local copies, waits for them, and re-layouts: 15.9 us -> 113 us
  matrix products: 83.4 us -> 70.4 us
    all_to_all x0 -> x1, waiting for transfers between devices: none -> 297 us  [body(): lax.all_to_all(jnp.stack([given] * lax.axis_size('col')), 'col', 0, 0)]
    all_gather x1 -> x0, waiting for transfers between devices: 110 us -> none  [body(): gathered = lax.all_gather(given, 'col', axis=1, tiled=True)]
    dynamic_update_slice x0 -> x32, local copies, waits for them, and re-layouts: none -> 52 us  [add_slot(): return lax.dynamic_update_slice(grid_now, current + product, place)]
    dynamic_slice x0 -> x32, local copies, waits for them, and re-layouts: none -> 17.6 us  [add_slot(): current = lax.dynamic_slice(grid_now, place, (basis_width, basis_width))]
    all_to_all x0 -> x1, local copies, waits for them, and re-layouts: none -> 17.6 us  [body(): lax.all_to_all(jnp.stack([given] * lax.axis_size('col')), 'col', 0, 0)]
    dot_general x16, matrix products: 45.9 us -> 32.8 us  [add_slot(): product = jnp.dot(left.T, applied, precision=lax.Precision.HIGHEST)]
    another operation x0 -> x1, local copies, waits for them, and re-layouts: none -> 7.9 us  [body(): jnp.stack([given] * lax.axis_size('col'))]
  transfers between devices with their start and end apart: 4 -> 4, of which waited for: 4 -> 4; matrix products, arithmetic and copies ran while one was open for 1% -> 0% of each run, Pallas kernels for 0% -> 0%
where the time goes in v1:
time: 729 us; the launch traced here: 722 us
  waiting for transfers between devices  456 us (63%)
  local copies, waits for them, and re-layouts  113 us (16%)
  matrix products  70.4 us (10%)
  loops' own time  50.3 us (7%)
  between operations  15.6 us (2%)
  other arithmetic  10.4 us (1%)
    all_to_all x1, waiting for transfers between devices, body(): lax.all_to_all(jnp.stack([given] * lax.axis_size('col')), 'col', 0, 0)  297 us
    all_gather x1, waiting for transfers between devices, body(): gathered = lax.all_gather(given, 'row', axis=0, tiled=True)  84.1 us
    dynamic_update_slice x32, local copies, waits for them, and re-layouts, add_slot(): return lax.dynamic_update_slice(grid_now, current + product, place)  52 us
    another operation x1, loops' own time, body(): local_grid = lax.fori_loop(0, tile_values.shape[0], add_slot, start_grid)  50.3 us
    all_gather x1, waiting for transfers between devices, body(): restrict_part = lax.all_gather(restrict_basis, 'col', axis=0, tiled=True)  45.2 us
    dot_general x16, matrix products, add_slot(): jnp.dot(tile_values[slot_index], right, precision=lax.Precision.HIGHEST)  37.6 us
    dot_general x16, matrix products, add_slot(): product = jnp.dot(left.T, applied, precision=lax.Precision.HIGHEST)  32.8 us
    all_gather x1, waiting for transfers between devices, body(): prolong_part = lax.all_gather(prolong_basis, 'row', axis=0, tiled=True)  28.3 us
  transfers between devices with their start and end apart: 4, of which 4 were waited for; matrix products, arithmetic and copies ran while one was open for 0% of the time, Pallas kernels for 0%

profile of v1, /device:TPU:1, one launch (start us, length us, event | category | flops | bytes accessed | tf_op | source)
XLA Modules:
  0.0 722.5 jit_solution(17819250476489276116)
XLA Ops:
  9.9 28.3 %all-gather.6.cloned.1.call-done = f32[2048,256]{1,0:T(8,128)} async-done(((f32[256,256]{1,0:T(8,128)}), f32[2048,256]{1,0:T(8,128)}) %all-gather.6.cloned.1.call-update) | async-done | bytes 2097168 | tf_op jit(solution)/shard_map/all_gather | solution.py:20
  38.2 45.2 %all-gather.4.cloned.1.call-done = f32[2048,256]{1,0:T(8,128)} async-done(((f32[128,256]{1,0:T(8,128)}), f32[2048,256]{1,0:T(8,128)}) %all-gather.4.cloned.1.call-update) | async-done | bytes 2097168 | tf_op jit(solution)/shard_map/all_gather | solution.py:19
  83.4 2.5 broadcast_in_dim.3.clone
  85.9 200.8 %while.13 = (s32[]{:T(128)}, f32[1024,1024]{0,1:T(8,128)}, s32[16,2]{0,1:T(2,128)S(1)}, s32[]{:T(128)}, f32[2048,256]{1,0:T(8,128)}, /*index=5*/f32[16,512,512]{...) while((s32[]{:T(128)}, f32[1024,1024]{0,1:T(8,128)}, ...), condition=%wide.region_1.2_spmd, body=%wide.region_0.1_spmd.sunk | while | flops 1208090624 | bytes 5767535 | solution.py:40
  95.3 2.9 dynamic_update_slice.8
  107.6 2.4 dynamic_update_slice.8
  119.5 3.6 dynamic_update_slice.8
  132.5 2.9 dynamic_update_slice.8
  144.8 3.6 dynamic_update_slice.8
  157.8 3.6 dynamic_update_slice.8
  170.8 3.6 dynamic_update_slice.8
  183.8 3.6 dynamic_update_slice.8
  208.6 3.5 dynamic_update_slice.8
  221.5 3.6 dynamic_update_slice.8
  234.6 3.6 dynamic_update_slice.8
  259.0 3.6 dynamic_update_slice.8
  272.0 2.9 dynamic_update_slice.8
  286.7 4.0 slice_select_fusion
  293.2 84.1 %all-gather.8.cloned.1.call-done = f32[4096,1024]{0,1:T(8,128)} async-done(((f32[512,1024]{0,1:T(8,128)}), f32[4096,1024]{0,1:T(8,128)}) %all-gather.8.cloned.1.call-update) | async-done | bytes 16777232 | tf_op jit(solution)/shard_map/all_gather | solution.py:51
  377.4 3.6 dynamic-slice_add_fusion
  383.7 7.9 %stack.2 = f32[16,512,512]{2,1,0:T(8,128)} broadcast(f32[512,512]{1,0:T(8,128)S(1)} %copy.10), dimensions={1,2} | broadcast | bytes 17825792 | tf_op jit(solution)/shard_map/stack | solution.py:57
  391.6 6.6 all-to-all-start
  398.8 296.6 %all-to-all-done = f32[16,512,512]{2,1,0:T(8,128)} async-done(((f32[16,512,512]{2,1,0:T(8,128)}), f32[16,512,512]{2,1,0:T(8,128)}, u32[]{:S(2)}, u32[]{:S(2)}) %all-to-all-start) | async-done | bytes 16777248 | tf_op jit(solution)/shard_map/all_to_all | solution.py:57
  695.5 17.6 %copy.11 = f32[16,512,512]{1,2,0:T(8,128)} copy(f32[16,512,512]{2,1,0:T(8,128)} %all-to-all-done) | data formatting | bytes 33554432 | tf_op jit(solution)/shard_map/all_to_all | solution.py:57
  (113 shorter events, 116.9 us)
Async XLA Ops:
  6.5 31.7 %all-gather.6.cloned.1.call-start = ((), (), s32[]{:S(2)}) async-start(), calls=%async_computation.2 | async-start | bytes 2359296 | tf_op jit(solution)/shard_map/all_gather | solution.py:20
  7.3 76.1 %all-gather.4.cloned.1.call-start = ((), (), s32[]{:S(2)}) async-start(), calls=%async_computation.1 | async-start | bytes 2228224 | tf_op jit(solution)/shard_map/all_gather | solution.py:19
  8.0 369.4 %all-gather.8.cloned.1.call-start = ((), (), s32[]{:S(2)}) async-start(), calls=%async_computation.3 | async-start | bytes 18874368 | tf_op jit(solution)/shard_map/all_gather | solution.py:51
  83.4 2.5 copy-start
  391.6 303.8 %all-to-all-start = ((f32[16,512,512]{2,1,0:T(8,128)}), f32[16,512,512]{2,1,0:T(8,128)}, u32[]{:S(2)}, u32[]{:S(2)}) async-start(f32[16,512,512]{2,1,0:T(8,128)} %stack.2), calls=%async_computation | async-start | bytes 33554432 | tf_op jit(solution)/shard_map/all_to_all | solution.py:57
Sparse Core Ops, SparseCore 0:
  9.0 29.1 all-gather.5
  40.3 43.0 all-gather.3
  290.9 86.4 all-gather.7
